TPU v7x, 256 devices: a whole 4x4x8 slice. The times are simulated.
256 devices in a mesh: bunch: 16 (over y, x), dom: 16 (over z, core).
Axes of the slice: x: 4, y: 4, z: 8, core: 2. Of those that a mesh axis runs over, the one named last changes fastest.
Arguments:
- particles: float32 [2, 64, 6, 32768], P(None, 'bunch', None, 'dom'), may hold values from -4.8 to 4.8
- slice_ids: int32 [2, 64, 32768], P(None, 'bunch', 'dom'), may hold values from 0 to 63
- maps: float32 [2, 8, 6, 6], replicated, may hold values from -1.3 to 1.3
- sextupoles: float32 [2, 8], replicated, may hold values from -0.05 to 0.05
Outputs:
- tracked: float32 [2, 64, 6, 32768], P(None, 'bunch', None, 'dom')
All inputs are finite; a program needn't handle non-finite values.
Results may differ from a plain program's by a relative error of at most 0.0003.
Values sent between devices are 32-bit elements; how exact they have to be, the bound alone decides.
A program may use at most 64 MiB of HBM per device.

v0:
```python
import jax
import jax.numpy as jnp
from jax import lax
from jax.sharding import PartitionSpec as P

SLICES = 64
SECTIONS = 8
TURNS = 2


kick_scale = 1.5
soft_width = 0.25


def from_behind(block, axis, distance):
    devices = range(lax.axis_size(axis))
    route = [((i - distance) % len(devices), i) for i in devices]
    return lax.ppermute(block, axis, route)


def features(coords):
    pos_x, mom_x, pos_y, mom_y, pos_z = (coords[0], coords[1], coords[2], coords[3], coords[4])
    return jnp.stack(
        [
            jnp.ones_like(pos_x),
            pos_x,
            mom_x,
            pos_y,
            mom_y,
            pos_z,
            pos_x * pos_x,
            pos_x * mom_x,
            mom_x * mom_x,
            pos_y * pos_y,
            pos_y * mom_y,
            mom_y * mom_y,
        ]
    )


def transport(coords, section_maps, strengths):
    moved = jnp.einsum("aij,abjp->abip", section_maps, coords, precision=lax.Precision.HIGHEST)
    pos_x = moved[:, :, 0]
    pos_y = moved[:, :, 2]
    factor = strengths[:, None, None]
    mom_x = moved[:, :, 1] + factor * (pos_x * pos_x - pos_y * pos_y)
    mom_y = moved[:, :, 3] - 2.0 * factor * pos_x * pos_y
    return jnp.stack([pos_x, mom_x, pos_y, mom_y, moved[:, :, 4], moved[:, :, 5]], axis=2)


def bunch_moments(coords, labels, slots):
    onehot = (labels[None, :] == slots).astype(jnp.float32)
    return lax.dot_general(
        features(coords), onehot, (((1,), (1,)), ((), ())), precision=lax.Precision.HIGHEST
    )


def kick_bunch(coords, opposing, population):
    counts = opposing[0]
    weight = counts / population
    inverse = 1.0 / jnp.maximum(counts, 1.0)
    cen_x = opposing[1] * inverse
    cen_px = opposing[2] * inverse
    cen_y = opposing[3] * inverse
    cen_py = opposing[4] * inverse
    cen_z = opposing[5] * inverse
    var_xx = opposing[6] * inverse - cen_x * cen_x
    var_xp = opposing[7] * inverse - cen_x * cen_px
    var_pp = opposing[8] * inverse - cen_px * cen_px
    var_yy = opposing[9] * inverse - cen_y * cen_y
    var_yq = opposing[10] * inverse - cen_y * cen_py
    var_qq = opposing[11] * inverse - cen_py * cen_py
    pos_x, mom_x, pos_y, mom_y, pos_z = (coords[0], coords[1], coords[2], coords[3], coords[4])
    drift = 0.5 * (pos_z[None, :] - cen_z[:, None])
    delta_x = pos_x[None, :] + drift * mom_x[None, :] - cen_x[:, None] - drift * cen_px[:, None]
    delta_y = pos_y[None, :] + drift * mom_y[None, :] - cen_y[:, None] - drift * cen_py[:, None]
    sigma_sq = (
        0.5
        * (
            var_xx[:, None]
            + 2.0 * drift * var_xp[:, None]
            + drift * drift * var_pp[:, None]
            + var_yy[:, None]
            + 2.0 * drift * var_yq[:, None]
            + drift * drift * var_qq[:, None]
        )
        + soft_width
    )
    strength = (
        weight[:, None]
        * jnp.exp(-(delta_x * delta_x + delta_y * delta_y) / (2.0 * sigma_sq))
        / sigma_sq
    )
    kick_x = jnp.sum(strength * delta_x, axis=0)
    kick_y = jnp.sum(strength * delta_y, axis=0)
    return jnp.stack(
        [pos_x, mom_x - kick_scale * kick_x, pos_y, mom_y - kick_scale * kick_y, pos_z, coords[5]]
    )


def partners(local_sums, offset):
    summed = lax.psum(local_sums, "dom")
    met_first = from_behind(summed[1], "bunch", offset)
    met_second = from_behind(summed[0], "bunch", -offset)
    opposing = jnp.stack([met_first, met_second])
    return opposing


def body(particles, slice_ids, maps, sextupoles):
    cycle_size = lax.axis_size("bunch")
    beams, bunches, comps, width = particles.shape
    population = float(width * lax.axis_size("dom"))
    labels = slice_ids.reshape(beams * bunches, width)
    slots = lax.broadcasted_iota(jnp.int32, (SLICES, width), 0)
    coords = particles
    for turn_index in range(TURNS):
        for section in range(SECTIONS):
            coords = transport(coords, maps[:, section], sextupoles[:, section])
            flattened = coords.reshape(beams * bunches, comps, width)
            local_sums = lax.map(
                lambda bundle: bunch_moments(bundle[0], bundle[1], slots), (flattened, labels)
            )
            local_sums = local_sums.reshape(beams, bunches, 12, SLICES)
            offset = (section + 1) % cycle_size
            opposing = partners(local_sums, offset).reshape(beams * bunches, 12, SLICES)
            kicked = lax.map(
                lambda bundle: kick_bunch(bundle[0], bundle[1], population), (flattened, opposing)
            )
            coords = kicked.reshape(beams, bunches, comps, width)
    return coords


def solution(mesh):
    return jax.shard_map(
        body,
        mesh=mesh,
        in_specs=(P(None, "bunch", None, "dom"), P(None, "bunch", "dom"), P(), P()),
        out_specs=P(None, "bunch", None, "dom"),
        check_vma=False,
    )
```

profile of v0, /device:TPU:9, one launch (start us, length us, event | category | flops | bytes accessed | tf_op | source)
XLA Modules:
  0.0 1166.2 jit_solution(4302759843659810641)
XLA Ops:
  5.3 5.8 while.384
  11.1 48.1 %psum.112 = f32[2,4,12,64]{3,2,1,0:T(8,128)S(1)} all-reduce(f32[2,4,12,64]{3,2,1,0:T(8,128)S(1)} %bitcast.2479), channel_id=1, replica_groups=mesh['bunch'=16,'dom'=16] {'dom'}, use_global_device_ids=true, to_apply=%region_2.3 | all-reduce | flops 6144 | bytes 49152 | tf_op jit(solution)/shard_map/psum | solution.py:102
  64.2 11.2 while.368
  77.0 5.8 while.385
  82.8 46.9 %psum.113 = f32[2,4,12,64]{3,2,1,0:T(8,128)S(1)} all-reduce(f32[2,4,12,64]{3,2,1,0:T(8,128)S(1)} %bitcast.2480), channel_id=1, replica_groups=mesh['bunch'=16,'dom'=16] {'dom'}, use_global_device_ids=true, to_apply=%region_9.10 | all-reduce | flops 6144 | bytes 49152 | tf_op jit(solution)/shard_map/psum | solution.py:102
  136.1 11.2 while.369
  148.9 5.8 while.386
  154.7 47.2 %psum.114 = f32[2,4,12,64]{3,2,1,0:T(8,128)S(1)} all-reduce(f32[2,4,12,64]{3,2,1,0:T(8,128)S(1)} %bitcast.2481), channel_id=1, replica_groups=mesh['bunch'=16,'dom'=16] {'dom'}, use_global_device_ids=true, to_apply=%region_16.17 | all-reduce | flops 6144 | bytes 49152 | tf_op jit(solution)/shard_map/psum | solution.py:102
  201.9 3.1 collective-permute-start.4
  206.1 3.0 collective-permute-done.5
  209.1 11.2 while.370
  221.9 5.8 while.387
  227.7 47.2 %psum.115 = f32[2,4,12,64]{3,2,1,0:T(8,128)S(1)} all-reduce(f32[2,4,12,64]{3,2,1,0:T(8,128)S(1)} %bitcast.2482), channel_id=1, replica_groups=mesh['bunch'=16,'dom'=16] {'dom'}, use_global_device_ids=true, to_apply=%region_23.24 | all-reduce | flops 6144 | bytes 49152 | tf_op jit(solution)/shard_map/psum | solution.py:102
  279.7 11.2 while.371
  292.4 5.8 while.388
  298.3 46.9 %psum.116 = f32[2,4,12,64]{3,2,1,0:T(8,128)S(1)} all-reduce(f32[2,4,12,64]{3,2,1,0:T(8,128)S(1)} %bitcast.2483), channel_id=1, replica_groups=mesh['bunch'=16,'dom'=16] {'dom'}, use_global_device_ids=true, to_apply=%region_30.31 | all-reduce | flops 6144 | bytes 49152 | tf_op jit(solution)/shard_map/psum | solution.py:102
  346.1 4.3 collective-permute-start.9
  351.7 11.2 while.372
  364.5 5.8 while.389
  370.3 46.9 %psum.117 = f32[2,4,12,64]{3,2,1,0:T(8,128)S(1)} all-reduce(f32[2,4,12,64]{3,2,1,0:T(8,128)S(1)} %bitcast.2484), channel_id=1, replica_groups=mesh['bunch'=16,'dom'=16] {'dom'}, use_global_device_ids=true, to_apply=%region_37.38 | all-reduce | flops 6144 | bytes 49152 | tf_op jit(solution)/shard_map/psum | solution.py:102
  419.0 4.1 collective-permute-start.11
  424.6 11.2 while.373
  437.3 5.8 while.390
  443.2 47.2 %psum.118 = f32[2,4,12,64]{3,2,1,0:T(8,128)S(1)} all-reduce(f32[2,4,12,64]{3,2,1,0:T(8,128)S(1)} %bitcast.2485), channel_id=1, replica_groups=mesh['bunch'=16,'dom'=16] {'dom'}, use_global_device_ids=true, to_apply=%region_44.45 | all-reduce | flops 6144 | bytes 49152 | tf_op jit(solution)/shard_map/psum | solution.py:102
  490.4 4.2 collective-permute-start.12
  494.6 3.5 collective-permute-start.13
  499.7 11.2 while.374
  512.5 5.8 while.391
  518.3 47.0 %psum.119 = f32[2,4,12,64]{3,2,1,0:T(8,128)S(1)} all-reduce(f32[2,4,12,64]{3,2,1,0:T(8,128)S(1)} %bitcast.2486), channel_id=1, replica_groups=mesh['bunch'=16,'dom'=16] {'dom'}, use_global_device_ids=true, to_apply=%region_51.52 | all-reduce | flops 6144 | bytes 49152 | tf_op jit(solution)/shard_map/psum | solution.py:102
  565.3 4.5 collective-permute-start.14
  571.1 3.1 collective-permute-done.15
  574.3 11.2 while.375
  587.1 5.8 while.392
  592.9 47.2 %psum.120 = f32[2,4,12,64]{3,2,1,0:T(8,128)S(1)} all-reduce(f32[2,4,12,64]{3,2,1,0:T(8,128)S(1)} %bitcast.2487), channel_id=1, replica_groups=mesh['bunch'=16,'dom'=16] {'dom'}, use_global_device_ids=true, to_apply=%region_58.59 | all-reduce | flops 6144 | bytes 49152 | tf_op jit(solution)/shard_map/psum | solution.py:102
  640.2 3.6 collective-permute-start.17
  645.1 11.2 while.376
  657.9 5.8 while.393
  663.7 46.9 %psum.121 = f32[2,4,12,64]{3,2,1,0:T(8,128)S(1)} all-reduce(f32[2,4,12,64]{3,2,1,0:T(8,128)S(1)} %bitcast.2488), channel_id=1, replica_groups=mesh['bunch'=16,'dom'=16] {'dom'}, use_global_device_ids=true, to_apply=%region_65.66 | all-reduce | flops 6144 | bytes 49152 | tf_op jit(solution)/shard_map/psum | solution.py:102
  710.7 4.0 collective-permute-start.19
  715.9 11.2 while.377
  728.7 5.8 while.394
  734.5 46.9 %psum.122 = f32[2,4,12,64]{3,2,1,0:T(8,128)S(1)} all-reduce(f32[2,4,12,64]{3,2,1,0:T(8,128)S(1)} %bitcast.2489), channel_id=1, replica_groups=mesh['bunch'=16,'dom'=16] {'dom'}, use_global_device_ids=true, to_apply=%region_72.73 | all-reduce | flops 6144 | bytes 49152 | tf_op jit(solution)/shard_map/psum | solution.py:102
  787.6 11.2 while.378
  800.4 5.8 while.395
  806.2 47.2 %psum.123 = f32[2,4,12,64]{3,2,1,0:T(8,128)S(1)} all-reduce(f32[2,4,12,64]{3,2,1,0:T(8,128)S(1)} %bitcast.2490), channel_id=1, replica_groups=mesh['bunch'=16,'dom'=16] {'dom'}, use_global_device_ids=true, to_apply=%region_79.80 | all-reduce | flops 6144 | bytes 49152 | tf_op jit(solution)/shard_map/psum | solution.py:102
  853.4 2.8 collective-permute-start.22
  859.3 11.2 while.379
  872.1 5.8 while.396
  878.0 47.2 %psum.124 = f32[2,4,12,64]{3,2,1,0:T(8,128)S(1)} all-reduce(f32[2,4,12,64]{3,2,1,0:T(8,128)S(1)} %bitcast.2491), channel_id=1, replica_groups=mesh['bunch'=16,'dom'=16] {'dom'}, use_global_device_ids=true, to_apply=%region_86.87 | all-reduce | flops 6144 | bytes 49152 | tf_op jit(solution)/shard_map/psum | solution.py:102
  925.5 4.8 collective-permute-start.25
  931.8 11.2 while.380
  944.6 5.8 while.397
  950.4 46.7 %psum.125 = f32[2,4,12,64]{3,2,1,0:T(8,128)S(1)} all-reduce(f32[2,4,12,64]{3,2,1,0:T(8,128)S(1)} %bitcast.2492), channel_id=1, replica_groups=mesh['bunch'=16,'dom'=16] {'dom'}, use_global_device_ids=true, to_apply=%region_93.94 | all-reduce | flops 6144 | bytes 49152 | tf_op jit(solution)/shard_map/psum | solution.py:102
  999.4 3.4 collective-permute-start.27
  1004.7 11.2 while.381
  1017.5 5.8 while.398
  1023.4 47.2 %psum.126 = f32[2,4,12,64]{3,2,1,0:T(8,128)S(1)} all-reduce(f32[2,4,12,64]{3,2,1,0:T(8,128)S(1)} %bitcast.2493), channel_id=1, replica_groups=mesh['bunch'=16,'dom'=16] {'dom'}, use_global_device_ids=true, to_apply=%region_100.101 | all-reduce | flops 6144 | bytes 49152 | tf_op jit(solution)/shard_map/psum | solution.py:102
  1070.5 4.2 collective-permute-start.28
  1079.7 11.2 while.382
  1092.5 5.8 while.399
  1098.3 47.2 %psum.127 = f32[2,4,12,64]{3,2,1,0:T(8,128)S(1)} all-reduce(f32[2,4,12,64]{3,2,1,0:T(8,128)S(1)} %bitcast.2494), channel_id=1, replica_groups=mesh['bunch'=16,'dom'=16] {'dom'}, use_global_device_ids=true, to_apply=%region_107.108 | all-reduce | flops 6144 | bytes 49152 | tf_op jit(solution)/shard_map/psum | solution.py:102
  1145.5 4.0 collective-permute-start.30
  1150.8 3.0 collective-permute-done.31
  1153.8 11.2 while.383
  (3012 shorter events, 331.7 us)
Async XLA Ops:
  0.0 3.0 copy-start
  3.9 0.8 copy-start.1
  59.2 5.0 collective-permute-start
  60.5 3.7 collective-permute-start.1
  129.7 5.2 collective-permute-start.2
  131.7 4.4 collective-permute-start.3
  201.9 4.2 collective-permute-start.4
  205.1 4.0 collective-permute-start.5
  274.9 3.1 collective-permute-start.6
  276.0 3.7 collective-permute-start.7
  345.2 6.5 collective-permute-start.8
  346.1 5.6 collective-permute-start.9
  417.2 6.7 collective-permute-start.10
  419.0 5.6 collective-permute-start.11
  490.4 9.1 collective-permute-start.12
  494.6 5.1 collective-permute-start.13
  565.3 5.8 collective-permute-start.14
  569.8 4.4 collective-permute-start.15
  640.1 5.0 collective-permute-start.16
  640.2 4.9 collective-permute-start.17
  710.6 5.2 collective-permute-start.18
  710.7 5.2 collective-permute-start.19
  781.4 5.4 collective-permute-start.20
  783.5 4.0 collective-permute-start.21
  853.4 3.8 collective-permute-start.22
  856.1 3.1 collective-permute-start.23
  925.2 6.6 collective-permute-start.24
  925.5 6.2 collective-permute-start.25
  997.2 6.7 collective-permute-start.26
  999.4 5.3 collective-permute-start.27
  1070.5 8.0 collective-permute-start.28
  1074.7 4.9 collective-permute-start.29
  1145.5 5.3 collective-permute-start.30
  1149.5 4.3 collective-permute-start.31
where the time goes:
time: 1180 us; the launch traced here: 1170 us
  blocking collectives  754 us (64%)
  other arithmetic  174 us (15%)
  starting transfers between devices  72.9 us (6%)
  local copies, waits for them, and re-layouts  55.3 us (5%)
  matrix products  54.5 us (5%)
  waiting for transfers between devices  34.7 us (3%)
  loops' own time  20 us (2%)
    psum x16, blocking collectives, partners(): summed = lax.psum(local_sums, 'dom')  754 us
    reduce_sum x128, other arithmetic, kick_bunch(): kick_y = jnp.sum(strength * delta_y, axis=0)  128 us
    ppermute x32, starting transfers between devices, from_behind(): return lax.ppermute(block, axis, route)  72.9 us
    dot_general x128, matrix products, bunch_moments(): lax.dot_general(features(coords), onehot, (((1,), (1,)), ((), ())), preci...  45.2 us
    ppermute x32, waiting for transfers between devices, from_behind(): return lax.ppermute(block, axis, route)  34.7 us
  transfers between devices with their start and end apart: 32, of which 27 were waited for; matrix products, arithmetic and copies ran while one was open for 0% of the time, Pallas kernels for 0%

commit v1 on v0

v1 whole, which is shorter than its diff:
```python
import functools
import math

import jax
import jax.numpy as jnp
from jax import lax
from jax.experimental import pallas as pl
from jax.experimental.pallas import tpu as pltpu
from jax.sharding import PartitionSpec as P

SLICES = 64
SECTIONS = 8
TURNS = 2
STEPS = SECTIONS * TURNS
MESH = pl.DeviceIdType.MESH

kick_scale = 1.5
soft_width = 0.25
CHUNK = 256
UNROLL = 4


def bf(value):
    return value.astype(jnp.bfloat16)


def split_rows(value):
    high = bf(value).astype(jnp.float32)
    return bf(jnp.concatenate([high, value - high], axis=0))


def slice_coefficients(sums, population):
    row = lax.broadcasted_iota(jnp.int32, (8, 128), 0)
    lane = lax.broadcasted_iota(jnp.int32, (8, 128), 1)
    low = lane < SLICES
    turned = pltpu.roll(sums, SLICES, 1)
    both = jnp.where(low, sums, turned)
    counts = jnp.where(low, turned, sums)
    inverse = 1.0 / jnp.maximum(counts, 1.0)
    mean = both * inverse
    cen_x, cen_px, cen_y, cen_py, cen_z, mean_rr, mean_rp, mean_pp = [
        jnp.broadcast_to(mean[r : r + 1], (8, 128)) for r in range(8)
    ]
    var_rr = mean_rr - cen_x * cen_x - cen_y * cen_y
    var_rp = mean_rp - cen_x * cen_px - cen_y * cen_py
    var_pp = mean_pp - cen_px * cen_px - cen_py * cen_py
    full = counts > 0.0
    scale = jnp.where(full, inverse * (population / (2.0 * kick_scale * math.log(2.0))), 0.0)
    scale_sq = (-2.0 * math.log(2.0)) * scale * scale
    half_z = 0.5 * cen_z
    cen = jnp.where(low, cen_x, cen_y)
    cen_p = jnp.where(low, cen_px, cen_py)
    first = jnp.where(low, 0, 2)
    zero = jnp.zeros((8, 128), jnp.float32)
    place = jnp.where(row == first, scale, zero)
    place = jnp.where(row == first + 1, -scale * half_z, place)
    place = jnp.where(row == 4, -0.5 * scale * cen_p, place)
    place = jnp.where(row == 6, -scale * (cen - half_z * cen_p), place)
    quad = 0.125 * var_pp
    line = 0.5 * var_rp - 0.25 * cen_z * var_pp
    const = soft_width + 0.5 * var_rr - half_z * var_rp + 0.5 * half_z * half_z * var_pp
    width = jnp.where(row == 4, scale_sq * line, zero)
    width = jnp.where(row == 5, scale_sq * quad, width)
    width = jnp.where(row == 6, jnp.where(full, scale_sq * const, -1.0), width)
    table = jnp.concatenate([place, width], axis=1)
    high = bf(table).astype(jnp.float32)
    rest = table - high
    stacked = jnp.concatenate([high, high, rest, rest], axis=0)
    return bf(jnp.transpose(stacked)[: 3 * SLICES])


def kernel(
    nb, nz, population,
    part_ref, ids_ref, maps_ref, sext_ref, out_ref,
    x_in, id_in, x_out, state, tiles, id_dense, onehot, counts, mom_rows, mom_bf, kick_rows, kick_bf, kick_x, kick_y,
    send_buf, recv_buf,
    send_sem, recv_sem, load_sem, swap_send, swap_recv, out_sem, out_send, out_recv,
):
    bunches, comps, width = part_ref.shape[1:]
    half_tiles = width // 128
    ntile = 2 * half_tiles
    groups = ntile // 8
    me = lax.axis_index("bunch")
    dom = lax.axis_index("dom")
    zed, core = lax.div(dom, 2), lax.rem(dom, 2)
    other = 1 - core
    peer = (me, 2 * zed + other)

    def partner_column(distance):
        return lax.rem(me + jnp.where(core == 0, nb - distance, distance), nb)

    own_x = pltpu.make_async_copy(part_ref.at[core], x_in.at[core], load_sem.at[0])
    own_id = pltpu.make_async_copy(ids_ref.at[core], id_in.at[core], load_sem.at[1])
    own_x.start()
    own_id.start()

    barrier = pltpu.get_barrier_semaphore()
    pl.semaphore_signal(barrier, inc=1, device_id=peer, device_id_type=MESH)

    def greet(n, carry):
        column = partner_column(lax.rem(lax.div(n, nz) + 1, nb))
        where = (column, 2 * lax.rem(n, nz) + other)
        pl.semaphore_signal(barrier, inc=1, device_id=where, device_id_type=MESH)
        return carry

    lax.fori_loop(0, SECTIONS * nz, greet, 0)
    pl.semaphore_wait(barrier, SECTIONS * nz + 1)

    swap_x = pltpu.make_async_remote_copy(
        src_ref=part_ref.at[other], dst_ref=x_in.at[core], send_sem=swap_send.at[0], recv_sem=swap_recv.at[0],
        device_id=peer, device_id_type=MESH,
    )
    swap_id = pltpu.make_async_remote_copy(
        src_ref=ids_ref.at[other], dst_ref=id_in.at[core], send_sem=swap_send.at[1], recv_sem=swap_recv.at[1],
        device_id=peer, device_id_type=MESH,
    )
    swap_id.start()
    swap_x.start()
    own_x.wait()
    own_id.wait()
    swap_id.wait()
    swap_x.wait()

    def unpack(i, carry):
        for h in range(2):
            for t in range(half_tiles):
                tiles[pl.ds((h * half_tiles + t) * 8, comps), :] = x_in[h, i, :, 128 * t : 128 * (t + 1)]
        for c in range(comps):
            for g in range(groups):
                state[i, c, 8 * g : 8 * g + 8, :] = tiles[pl.ds(64 * g + c, 8, stride=8), :]
        return carry

    lax.fori_loop(0, bunches, unpack, 0)
    for h in range(2):
        for t in range(half_tiles):
            tiles[pl.ds((h * half_tiles + t) * 8, bunches), :] = id_in[h, :, 128 * t : 128 * (t + 1)].astype(jnp.float32)
    for i in range(bunches):
        for g in range(groups):
            id_dense[i, 8 * g : 8 * g + 8, :] = tiles[pl.ds(64 * g + i, 8, stride=8), :]

    mom_bf[...] = jnp.ones(mom_bf.shape, jnp.bfloat16)
    slot = (lax.broadcasted_iota(jnp.int32, (128, 128), 1) & (SLICES - 1)).astype(jnp.float32)

    def build(i, carry):
        columns = jnp.transpose(id_dense[i])
        for t in range(ntile):
            onehot[i, 128 * t : 128 * (t + 1), :] = bf(
                jnp.where(columns[:, t : t + 1] == slot, 1.0, 0.0)
            )
        counts[i] = jnp.dot(mom_bf[...], onehot[i], preferred_element_type=jnp.float32)[:8]
        return carry

    lax.fori_loop(0, bunches, build, 0)

    for g in range(groups):
        kick_rows[pl.ds(64 * g + 7, 8, stride=8), :] = jnp.zeros((8, 128), jnp.float32)
    low = lax.broadcasted_iota(jnp.int32, (8, 128), 1) < SLICES
    one = jnp.ones((8, 128), jnp.float32)

    def advance(step, i):
        section = lax.rem(step, SECTIONS)
        at = core * SECTIONS + section
        base = at * comps * comps
        cell = [[maps_ref[base + comps * r + c] for c in range(comps)] for r in range(comps)]
        strength = sext_ref[at]
        for g in range(groups):
            rows = slice(8 * g, 8 * g + 8)
            old = [state[i, c, rows, :] for c in range(comps)]
            new = []
            for r in range(comps):
                total = cell[r][0] * old[0]
                for c in range(1, comps):
                    total = total + cell[r][c] * old[c]
                new.append(total)
            x, px, y, py, z, dp = new
            px = px + strength * (x * x - y * y)
            py = py - 2.0 * strength * (x * y)
            for c, value in enumerate((x, px, y, py, z, dp)):
                state[i, c, rows, :] = value
            half = 0.5 * z
            mom = (x, px, y, py, z, x * x + y * y, x * px + y * py, px * px + py * py)
            kick = (x + half * px, px, y + half * py, py, z, z * z, one)
            for f, value in enumerate(mom):
                mom_rows[pl.ds(64 * g + f, 8, stride=8), :] = value
            for f, value in enumerate(kick):
                kick_rows[pl.ds(64 * g + f, 8, stride=8), :] = value
        for t in range(ntile):
            lanes = slice(128 * t, 128 * (t + 1))
            mom_bf[:, lanes] = split_rows(mom_rows[8 * t : 8 * t + 8, :])
            kick_bf[i, :, lanes] = split_rows(kick_rows[8 * t : 8 * t + 8, :])
        sums = jnp.dot(mom_bf[...], onehot[i], preferred_element_type=jnp.float32)
        n = step * bunches + i
        send_buf[n] = jnp.where(low, sums[:8] + sums[8:], counts[i])
        column = partner_column(lax.rem(section + 1, nb))

        def send(r, carry):
            pltpu.make_async_remote_copy(
                src_ref=send_buf.at[n], dst_ref=recv_buf.at[n, zed], send_sem=send_sem.at[n], recv_sem=recv_sem.at[n],
                device_id=(column, 2 * lax.rem(zed + r, nz) + other), device_id_type=MESH,
            ).start()
            return carry

        lax.fori_loop(0, nz, send, 0)

    def kick(step, i):
        n = step * bunches + i
        pltpu.make_async_copy(recv_buf.at[n], recv_buf.at[n], recv_sem.at[n]).wait()
        sums = recv_buf[n, 0]
        for r in range(1, nz):
            sums = sums + recv_buf[n, r]
        table = slice_coefficients(sums, population)

        def chunk(m):
            start = m * CHUNK
            if not isinstance(start, int):
                start = pl.multiple_of(start, CHUNK)
            part = kick_bf[i, :, pl.ds(start, CHUNK)]
            made = jnp.dot(table, jnp.concatenate([part, part], axis=0), preferred_element_type=jnp.float32)
            dx, dy, width_neg = made[:SLICES], made[SLICES : 2 * SLICES], made[2 * SLICES :]
            recip = 1.0 / width_neg
            factor = jnp.exp2((dx * dx + dy * dy) * recip) * recip
            for ref, delta in ((kick_x, dx), (kick_y, dy)):
                term = factor * delta
                total = term[:8]
                for j in range(8, SLICES, 8):
                    total = total + term[j : j + 8]
                for u in range(CHUNK // 128):
                    ref[pl.ds(pl.multiple_of((m * (CHUNK // 128) + u) * 8, 8), 8), :] = total[:, 128 * u : 128 * (u + 1)]

        def chunks(q, carry):
            for u in range(UNROLL):
                chunk(q * UNROLL + u)
            return carry

        lax.fori_loop(0, ntile * 128 // (CHUNK * UNROLL), chunks, 0)
        for c, ref in ((1, kick_x), (3, kick_y)):
            for g in range(groups):
                total = state[i, c, 8 * g : 8 * g + 8, :]
                for r in range(8):
                    total = total + ref[pl.ds(64 * g + r, 8, stride=8), :]
                state[i, c, 8 * g : 8 * g + 8, :] = total

    def enter(i, carry):
        advance(0, i)
        return carry

    lax.fori_loop(0, bunches, enter, 0)

    def cycle(n, carry):
        step, i = lax.div(n, bunches), lax.rem(n, bunches)
        kick(step, i)
        advance(step + 1, i)
        return carry

    lax.fori_loop(0, (STEPS - 1) * bunches, cycle, 0)

    def leave(i, carry):
        kick(STEPS - 1, i)
        for c in range(comps):
            for g in range(groups):
                tiles[pl.ds(64 * g + c, 8, stride=8), :] = state[i, c, 8 * g : 8 * g + 8, :]
        for h in range(2):
            for t in range(half_tiles):
                x_out[h, i, :, 128 * t : 128 * (t + 1)] = tiles[pl.ds((h * half_tiles + t) * 8, comps), :]
        own_out(i).start()
        swap_out(i).start()
        return carry

    def own_out(i):
        return pltpu.make_async_copy(x_out.at[core, i], out_ref.at[core, i], out_sem.at[i])

    def swap_out(i):
        return pltpu.make_async_remote_copy(
            src_ref=x_out.at[other, i], dst_ref=out_ref.at[core, i], send_sem=out_send.at[i], recv_sem=out_recv.at[i],
            device_id=peer, device_id_type=MESH,
        )

    lax.fori_loop(0, bunches, leave, 0)

    def finish(i, carry):
        own_out(i).wait()
        swap_out(i).wait()
        return carry

    def drain(n, carry):
        pltpu.make_async_copy(recv_buf.at[n], recv_buf.at[n], send_sem.at[n]).wait()
        return carry

    lax.fori_loop(0, STEPS * bunches, drain, 0)
    lax.fori_loop(0, bunches, finish, 0)


def body(particles, slice_ids, maps, sextupoles):
    nb, nd = lax.axis_size("bunch"), lax.axis_size("dom")
    nz = nd // 2
    beams, bunches, comps, width = particles.shape
    ntile = 2 * width // 128
    slots = STEPS * bunches
    f32, b16 = jnp.float32, jnp.bfloat16
    vmem, dma = pltpu.VMEM, pltpu.SemaphoreType.DMA
    return pl.pallas_call(
        functools.partial(kernel, nb, nz, float(width * nd)),
        out_shape=jax.ShapeDtypeStruct(particles.shape, f32),
        in_specs=[
            pl.BlockSpec(memory_space=pl.ANY),
            pl.BlockSpec(memory_space=pl.ANY),
            pl.BlockSpec(memory_space=pltpu.SMEM),
            pl.BlockSpec(memory_space=pltpu.SMEM),
        ],
        out_specs=pl.BlockSpec(memory_space=pl.ANY),
        scratch_shapes=[
            vmem((2, bunches, comps, width), f32),
            vmem((2, bunches, width), jnp.int32),
            vmem((2, bunches, comps, width), f32),
            vmem((bunches, comps, ntile, 128), f32),
            vmem((8 * ntile, 128), f32),
            vmem((bunches, ntile, 128), f32),
            vmem((bunches, 2 * width, 128), b16),
            vmem((bunches, 8, 128), f32),
            vmem((8 * ntile, 128), f32),
            vmem((16, 2 * width), b16),
            vmem((8 * ntile, 128), f32),
            vmem((bunches, 16, 2 * width), b16),
            vmem((8 * ntile, 128), f32),
            vmem((8 * ntile, 128), f32),
            vmem((slots, 8, 128), f32),
            vmem((slots, nz, 8, 128), f32),
            dma((slots,)),
            dma((slots,)),
            dma((2,)),
            dma((2,)),
            dma((2,)),
            dma((bunches,)),
            dma((bunches,)),
            dma((bunches,)),
        ],
        compiler_params=pltpu.CompilerParams(
            collective_id=0, has_side_effects=True, vmem_limit_bytes=40 << 20
        ),
        name="track",
    )(particles, slice_ids, maps.reshape(-1), sextupoles.reshape(-1))


def solution(mesh):
    return jax.shard_map(
        body,
        mesh=mesh,
        in_specs=(P(None, "bunch", None, "dom"), P(None, "bunch", "dom"), P(), P()),
        out_specs=P(None, "bunch", None, "dom"),
        check_vma=False,
    )
```

time: 1180 us -> 155 us (0.13); the launches traced: 1170 us -> 154 us
  blocking collectives: 754 us -> 0 us
  other arithmetic: 174 us -> 0 us
  Pallas kernels: 0 us -> 150 us
  starting transfers between devices: 72.9 us -> 0 us
  matrix products: 54.5 us -> 0 us
  local copies, waits for them, and re-layouts: 55.3 us -> 4.08 us
  waiting for transfers between devices: 34.7 us -> 0 us
  loops' own time: 20 us -> 0 us
    psum x16 -> x0, blocking collectives: 754 us -> none  [partners(): summed = lax.psum(local_sums, 'dom')]
    pallas_call x0 -> x1, Pallas kernels: none -> 150 us  [body(): pl.pallas_call(functools.partial(kernel, nb, nz, float(width * nd)), out_...]
    reduce_sum x128 -> x0, other arithmetic: 128 us -> none  [kick_bunch(): kick_y = jnp.sum(strength * delta_y, axis=0)]
    ppermute x32 -> x0, starting transfers between devices: 72.9 us -> none  [from_behind(): return lax.ppermute(block, axis, route)]
    dot_general x144 -> x0, matrix products: 54.5 us -> none  [the longest x128 45.2 us: bunch_moments(): lax.dot_general(features(coords), onehot, (((1,), (1,)), ((), ())), preci...]
    another operation x432 -> x0, local copies, waits for them, and re-layouts: 42.9 us -> none  [the longest x128 21.6 us: features(): jnp.stack([jnp.ones_like(pos_x), pos_x, mom_x, pos_y, mom_y, pos_z, pos_x...]
    ppermute x32 -> x0, waiting for transfers between devices: 34.7 us -> none  [from_behind(): return lax.ppermute(block, axis, route)]
    another operation x32 -> x0, loops' own time: 20 us -> none  [the longest x16 11.6 us: body(): lax.map(lambda bundle: kick_bunch(bundle[0], bundle[1], population), (fla...]
  transfers between devices with their start and end apart: 32 -> 0, of which waited for: 27 -> 0; matrix products, arithmetic and copies ran while one was open for 0% -> 0% of each run, Pallas kernels for 0% -> 0%
where the time goes in v1:
time: 155 us; the launch traced here: 154 us
  Pallas kernels  150 us (97%)
  local copies, waits for them, and re-layouts  4.08 us (3%)
    pallas_call x1, Pallas kernels, body(): pl.pallas_call(functools.partial(kernel, nb, nz, float(width * nd)), out_...  150 us

profile of v1, /device:TPU:9, one launch (start us, length us, event | category | flops | bytes accessed | tf_op | source)
XLA Modules:
  0.0 153.9 jit_solution(9189845113067752015)
XLA Ops:
  0.0 0.8 reshape.7.sext_ref
  0.8 0.9 copy.7
  1.7 0.1 reshape.6.maps_ref
  1.8 0.0 copy-start
  1.8 1.3 copy.8.part_ref
  3.1 0.0 copy-done
  3.1 149.8 %track.1 = f32[2,4,6,2048]{3,2,1,0:T(8,128)S(1)} custom-call(f32[2,4,6,2048]{3,2,1,0:T(8,128)S(1)} %copy.8.part_ref, s32[2,4,2048]{2,1,0:T(4,128)S(1)} %copy-done, f32[576]{0:T(1024)S(1)} %reshape.6.maps_ref, f32[16]{0:T(128)S(1)} %reshape.7.sext_ref), custom_call_target="tpu_custom_call" | custom-call | tf_op jit(solution)/shard_map/track/pallas_call | solution.py:301
  152.9 1.0 copy.9
Async XLA Ops:
  1.8 1.3 copy-start

commit v2 on v1

--- a/solution.py
+++ b/solution.py
@@ -16,8 +16,8 @@
 
 kick_scale = 1.5
 soft_width = 0.25
-CHUNK = 256
-UNROLL = 4
+CHUNK = 128
+ROWS = 5
 
 
 def bf(value):
@@ -33,13 +33,15 @@
     row = lax.broadcasted_iota(jnp.int32, (8, 128), 0)
     lane = lax.broadcasted_iota(jnp.int32, (8, 128), 1)
     low = lane < SLICES
-    turned = pltpu.roll(sums, SLICES, 1)
-    both = jnp.where(low, sums, turned)
-    counts = jnp.where(low, turned, sums)
+    counts = jnp.broadcast_to(sums[4:5], (8, 128))
     inverse = 1.0 / jnp.maximum(counts, 1.0)
-    mean = both * inverse
-    cen_x, cen_px, cen_y, cen_py, cen_z, mean_rr, mean_rp, mean_pp = [
-        jnp.broadcast_to(mean[r : r + 1], (8, 128)) for r in range(8)
+    mean = sums[:4] * inverse[:4]
+    turned = pltpu.roll(mean, SLICES, 1)
+    cen_x, cen_px, cen_y, cen_py = [
+        jnp.broadcast_to(r, (8, 128)) for r in jnp.split(jnp.where(low[:4], mean, turned), 4)
+    ]
+    cen_z, mean_rr, mean_rp, mean_pp = [
+        jnp.broadcast_to(r, (8, 128)) for r in jnp.split(jnp.where(low[:4], turned, mean), 4)
     ]
     var_rr = mean_rr - cen_x * cen_x - cen_y * cen_y
     var_rp = mean_rp - cen_x * cen_px - cen_y * cen_py
@@ -66,14 +68,16 @@
     high = bf(table).astype(jnp.float32)
     rest = table - high
     stacked = jnp.concatenate([high, high, rest, rest], axis=0)
-    return bf(jnp.transpose(stacked)[: 3 * SLICES])
+    turned = jnp.transpose(stacked)
+    order = [turned[j + SLICES * f : j + SLICES * f + 8] for j in range(0, SLICES, 8) for f in range(3)]
+    return bf(jnp.concatenate(order, axis=0))
 
 
 def kernel(
     nb, nz, population,
     part_ref, ids_ref, maps_ref, sext_ref, out_ref,
     x_in, id_in, x_out, state, tiles, id_dense, onehot, counts, mom_rows, mom_bf, kick_rows, kick_bf, kick_x, kick_y,
-    send_buf, recv_buf,
+    send_buf, recv_buf, ahead,
     send_sem, recv_sem, load_sem, swap_send, swap_recv, out_sem, out_send, out_recv,
 ):
     bunches, comps, width = part_ref.shape[1:]
@@ -97,13 +101,13 @@
     barrier = pltpu.get_barrier_semaphore()
     pl.semaphore_signal(barrier, inc=1, device_id=peer, device_id_type=MESH)
 
-    def greet(n, carry):
-        column = partner_column(lax.rem(lax.div(n, nz) + 1, nb))
-        where = (column, 2 * lax.rem(n, nz) + other)
-        pl.semaphore_signal(barrier, inc=1, device_id=where, device_id_type=MESH)
-        return carry
-
-    lax.fori_loop(0, SECTIONS * nz, greet, 0)
+    def greet(k, carry):
+        column = partner_column(lax.rem(k + 1, nb))
+        for r in range(nz):
+            pl.semaphore_signal(barrier, inc=1, device_id=(column, 2 * r + other), device_id_type=MESH)
+        return carry
+
+    lax.fori_loop(0, SECTIONS, greet, 0)
     pl.semaphore_wait(barrier, SECTIONS * nz + 1)
 
     swap_x = pltpu.make_async_remote_copy(
@@ -157,125 +161,141 @@
     low = lax.broadcasted_iota(jnp.int32, (8, 128), 1) < SLICES
     one = jnp.ones((8, 128), jnp.float32)
 
-    def advance(step, i):
-        section = lax.rem(step, SECTIONS)
-        at = core * SECTIONS + section
-        base = at * comps * comps
-        cell = [[maps_ref[base + comps * r + c] for c in range(comps)] for r in range(comps)]
-        strength = sext_ref[at]
+    def cells(step):
+        base = (core * SECTIONS + lax.rem(step, SECTIONS)) * comps * comps
+        return [[maps_ref[base + comps * r + c] for c in range(comps)] for r in range(comps)]
+
+    def prepare(step, i):
+        cell = cells(step)
         for g in range(groups):
             rows = slice(8 * g, 8 * g + 8)
             old = [state[i, c, rows, :] for c in range(comps)]
-            new = []
             for r in range(comps):
                 total = cell[r][0] * old[0]
                 for c in range(1, comps):
                     total = total + cell[r][c] * old[c]
-                new.append(total)
+                ahead[r, rows, :] = total
+
+    def gathered(ref, g):
+        total = ref[pl.ds(64 * g, 8, stride=8), :]
+        for r in range(1, 8):
+            total = total + ref[pl.ds(64 * g + r, 8, stride=8), :]
+        return total
+
+    def advance(step, i, kicked):
+        cell = cells(step)
+        strength = sext_ref[core, lax.rem(step, SECTIONS)]
+        for g in range(groups):
+            rows = slice(8 * g, 8 * g + 8)
+            new = [ahead[r, rows, :] for r in range(comps)]
+            if kicked:
+                add_x, add_y = gathered(kick_x, g), gathered(kick_y, g)
+                new = [new[r] + (cell[r][1] * add_x + cell[r][3] * add_y) for r in range(comps)]
             x, px, y, py, z, dp = new
-            px = px + strength * (x * x - y * y)
+            xx, yy = x * x, y * y
+            px = px + strength * (xx - yy)
             py = py - 2.0 * strength * (x * y)
             for c, value in enumerate((x, px, y, py, z, dp)):
                 state[i, c, rows, :] = value
             half = 0.5 * z
-            mom = (x, px, y, py, z, x * x + y * y, x * px + y * py, px * px + py * py)
+            mom = (x, px, y, py, z, xx + yy, x * px + y * py, px * px + py * py)
             kick = (x + half * px, px, y + half * py, py, z, z * z, one)
             for f, value in enumerate(mom):
                 mom_rows[pl.ds(64 * g + f, 8, stride=8), :] = value
             for f, value in enumerate(kick):
                 kick_rows[pl.ds(64 * g + f, 8, stride=8), :] = value
         for t in range(ntile):
-            lanes = slice(128 * t, 128 * (t + 1))
-            mom_bf[:, lanes] = split_rows(mom_rows[8 * t : 8 * t + 8, :])
-            kick_bf[i, :, lanes] = split_rows(kick_rows[8 * t : 8 * t + 8, :])
+            mom_bf[:, 128 * t : 128 * (t + 1)] = split_rows(mom_rows[8 * t : 8 * t + 8, :])
         sums = jnp.dot(mom_bf[...], onehot[i], preferred_element_type=jnp.float32)
+        sums = sums[:8] + sums[8:]
+        send_buf[step * bunches + i] = jnp.concatenate(
+            [jnp.where(low[:4], sums[:4], sums[4:]), counts[i, :4, :]], axis=0
+        )
+
+    def features(i):
+        for t in range(ntile):
+            kick_bf[i, :, 128 * t : 128 * (t + 1)] = split_rows(kick_rows[8 * t : 8 * t + 8, :])
+
+    def send(step, i):
         n = step * bunches + i
-        send_buf[n] = jnp.where(low, sums[:8] + sums[8:], counts[i])
-        column = partner_column(lax.rem(section + 1, nb))
-
-        def send(r, carry):
+        column = partner_column(lax.rem(lax.rem(step, SECTIONS) + 1, nb))
+        for r in sorted(range(nz), key=lambda r: -min(r, nz - r)):
             pltpu.make_async_remote_copy(
-                src_ref=send_buf.at[n], dst_ref=recv_buf.at[n, zed], send_sem=send_sem.at[n], recv_sem=recv_sem.at[n],
+                src_ref=send_buf.at[n, pl.ds(0, ROWS)], dst_ref=recv_buf.at[n, zed, pl.ds(0, ROWS)],
+                send_sem=send_sem.at[n], recv_sem=recv_sem.at[n],
                 device_id=(column, 2 * lax.rem(zed + r, nz) + other), device_id_type=MESH,
             ).start()
-            return carry
-
-        lax.fori_loop(0, nz, send, 0)
-
-    def kick(step, i):
+
+    def meet(step, i):
         n = step * bunches + i
-        pltpu.make_async_copy(recv_buf.at[n], recv_buf.at[n], recv_sem.at[n]).wait()
-        sums = recv_buf[n, 0]
+        landed = recv_buf.at[n, :, pl.ds(0, ROWS)]
+        pltpu.make_async_copy(landed, landed, recv_sem.at[n]).wait()
+        sums = recv_buf[n, 0, :ROWS]
         for r in range(1, nz):
-            sums = sums + recv_buf[n, r]
-        table = slice_coefficients(sums, population)
-
-        def chunk(m):
-            start = m * CHUNK
-            if not isinstance(start, int):
-                start = pl.multiple_of(start, CHUNK)
-            part = kick_bf[i, :, pl.ds(start, CHUNK)]
-            made = jnp.dot(table, jnp.concatenate([part, part], axis=0), preferred_element_type=jnp.float32)
-            dx, dy, width_neg = made[:SLICES], made[SLICES : 2 * SLICES], made[2 * SLICES :]
-            recip = 1.0 / width_neg
-            factor = jnp.exp2((dx * dx + dy * dy) * recip) * recip
-            for ref, delta in ((kick_x, dx), (kick_y, dy)):
-                term = factor * delta
-                total = term[:8]
-                for j in range(8, SLICES, 8):
-                    total = total + term[j : j + 8]
-                for u in range(CHUNK // 128):
-                    ref[pl.ds(pl.multiple_of((m * (CHUNK // 128) + u) * 8, 8), 8), :] = total[:, 128 * u : 128 * (u + 1)]
-
-        def chunks(q, carry):
-            for u in range(UNROLL):
-                chunk(q * UNROLL + u)
-            return carry
-
-        lax.fori_loop(0, ntile * 128 // (CHUNK * UNROLL), chunks, 0)
-        for c, ref in ((1, kick_x), (3, kick_y)):
-            for g in range(groups):
-                total = state[i, c, 8 * g : 8 * g + 8, :]
-                for r in range(8):
-                    total = total + ref[pl.ds(64 * g + r, 8, stride=8), :]
-                state[i, c, 8 * g : 8 * g + 8, :] = total
-
-    def enter(i, carry):
-        advance(0, i)
-        return carry
-
-    lax.fori_loop(0, bunches, enter, 0)
-
-    def cycle(n, carry):
-        step, i = lax.div(n, bunches), lax.rem(n, bunches)
-        kick(step, i)
-        advance(step + 1, i)
-        return carry
-
-    lax.fori_loop(0, (STEPS - 1) * bunches, cycle, 0)
-
-    def leave(i, carry):
-        kick(STEPS - 1, i)
+            sums = sums + recv_buf[n, r, :ROWS]
+        return slice_coefficients(sums, population)
+
+    def chunk(table, i, m):
+        part = kick_bf[i, :, CHUNK * m : CHUNK * (m + 1)]
+        made = jnp.dot(table, jnp.concatenate([part, part], axis=0), preferred_element_type=jnp.float32)
+        for u in range(CHUNK // 128):
+            lanes = slice(128 * u, 128 * (u + 1))
+            total_x = total_y = None
+            for j in range(0, SLICES, 8):
+                dx = made[3 * j : 3 * j + 8, lanes]
+                dy = made[3 * j + 8 : 3 * j + 16, lanes]
+                recip = 1.0 / made[3 * j + 16 : 3 * j + 24, lanes]
+                factor = jnp.exp2((dx * dx + dy * dy) * recip) * recip
+                total_x = factor * dx if j == 0 else total_x + factor * dx
+                total_y = factor * dy if j == 0 else total_y + factor * dy
+            row = (m * (CHUNK // 128) + u) * 8
+            kick_x[row : row + 8, :] = total_x
+            kick_y[row : row + 8, :] = total_y
+
+    def slot(step, i):
+        table = meet(step, i)
+        for m in range(ntile * 128 // CHUNK):
+            chunk(table, i, m)
+
+    for i in range(bunches):
+        prepare(0, i)
+        advance(0, i, False)
+        send(0, i)
+        features(i)
+
+    def cycle(step, carry):
+        for i in range(bunches):
+            prepare(step + 1, i)
+            slot(step, i)
+            advance(step + 1, i, True)
+            send(step + 1, i)
+            features(i)
+        return carry
+
+    lax.fori_loop(0, STEPS - 1, cycle, 0)
+
+    def own_out(i):
+        return pltpu.make_async_copy(x_out.at[core, i], out_ref.at[core, i], out_sem.at[i])
+
+    def swap_out(i):
+        return pltpu.make_async_remote_copy(
+            src_ref=x_out.at[other, i], dst_ref=out_ref.at[core, i], send_sem=out_send.at[i], recv_sem=out_recv.at[i],
+            device_id=peer, device_id_type=MESH,
+        )
+
+    for i in range(bunches):
+        slot(STEPS - 1, i)
         for c in range(comps):
             for g in range(groups):
-                tiles[pl.ds(64 * g + c, 8, stride=8), :] = state[i, c, 8 * g : 8 * g + 8, :]
+                value = state[i, c, 8 * g : 8 * g + 8, :]
+                if c in (1, 3):
+                    value = value + gathered(kick_x if c == 1 else kick_y, g)
+                tiles[pl.ds(64 * g + c, 8, stride=8), :] = value
         for h in range(2):
             for t in range(half_tiles):
                 x_out[h, i, :, 128 * t : 128 * (t + 1)] = tiles[pl.ds((h * half_tiles + t) * 8, comps), :]
         own_out(i).start()
         swap_out(i).start()
-        return carry
-
-    def own_out(i):
-        return pltpu.make_async_copy(x_out.at[core, i], out_ref.at[core, i], out_sem.at[i])
-
-    def swap_out(i):
-        return pltpu.make_async_remote_copy(
-            src_ref=x_out.at[other, i], dst_ref=out_ref.at[core, i], send_sem=out_send.at[i], recv_sem=out_recv.at[i],
-            device_id=peer, device_id_type=MESH,
-        )
-
-    lax.fori_loop(0, bunches, leave, 0)
 
     def finish(i, carry):
         own_out(i).wait()
@@ -283,7 +303,8 @@
         return carry
 
     def drain(n, carry):
-        pltpu.make_async_copy(recv_buf.at[n], recv_buf.at[n], send_sem.at[n]).wait()
+        landed = recv_buf.at[n, :, pl.ds(0, ROWS)]
+        pltpu.make_async_copy(landed, landed, send_sem.at[n]).wait()
         return carry
 
     lax.fori_loop(0, STEPS * bunches, drain, 0)
@@ -302,8 +323,8 @@
         functools.partial(kernel, nb, nz, float(width * nd)),
         out_shape=jax.ShapeDtypeStruct(particles.shape, f32),
         in_specs=[
-            pl.BlockSpec(memory_space=pl.ANY),
-            pl.BlockSpec(memory_space=pl.ANY),
+            pl.BlockSpec(memory_space=pltpu.HBM),
+            pl.BlockSpec(memory_space=pltpu.HBM),
             pl.BlockSpec(memory_space=pltpu.SMEM),
             pl.BlockSpec(memory_space=pltpu.SMEM),
         ],
@@ -325,6 +346,7 @@
             vmem((8 * ntile, 128), f32),
             vmem((slots, 8, 128), f32),
             vmem((slots, nz, 8, 128), f32),
+            vmem((comps, ntile, 128), f32),
             dma((slots,)),
             dma((slots,)),
             dma((2,)),
@@ -338,7 +360,7 @@
             collective_id=0, has_side_effects=True, vmem_limit_bytes=40 << 20
         ),
         name="track",
-    )(particles, slice_ids, maps.reshape(-1), sextupoles.reshape(-1))
+    )(particles, slice_ids, maps.reshape(-1), sextupoles)
 
 
 def solution(mesh):

time: 155 us -> 133 us (0.86)
  Pallas kernels: 150 us -> 129 us
    pallas_call x1, Pallas kernels: 150 us -> 129 us  [body(): pl.pallas_call(functools.partial(kernel, nb, nz, float(width * nd)), out_...]
where the time goes in v2:
time: 133 us
  Pallas kernels  129 us (97%)
  local copies, waits for them, and re-layouts  3.33 us (3%)
    pallas_call x1, Pallas kernels, body(): pl.pallas_call(functools.partial(kernel, nb, nz, float(width * nd)), out_...  129 us

profile of v2, /device:TPU:9, one launch (start us, length us, event | category | flops | bytes accessed | tf_op | source)
XLA Modules:
  0.0 132.8 jit_solution(11077268262730366547)
XLA Ops:
  0.0 0.9 copy.7
  0.9 0.1 reshape.3.maps_ref
  1.1 0.0 copy-start
  1.1 0.0 copy-start.1
  1.1 1.3 copy.8.part_ref
  2.3 0.0 copy-done
  2.4 0.0 copy-done.1
  2.4 129.4 %track.1 = f32[2,4,6,2048]{3,2,1,0:T(8,128)S(1)} custom-call(f32[2,4,6,2048]{3,2,1,0:T(8,128)S(1)} %copy.8.part_ref, s32[2,4,2048]{2,1,0:T(4,128)S(1)} %copy-done, f32[576]{0:T(1024)S(1)} %reshape.3.maps_ref, f32[2,8]{1,0:T(2,128)S(1)} %copy-done.1), custom_call_target="tpu_custom_call" | custom-call | tf_op jit(solution)/shard_map/track/pallas_call | solution.py:322
  131.8 1.0 copy.9
Async XLA Ops:
  1.1 1.3 copy-start
  1.1 1.3 copy-start.1

commit v3 on v2

--- a/solution.py
+++ b/solution.py
@@ -93,8 +93,8 @@
     def partner_column(distance):
         return lax.rem(me + jnp.where(core == 0, nb - distance, distance), nb)
 
-    own_x = pltpu.make_async_copy(part_ref.at[core], x_in.at[core], load_sem.at[0])
-    own_id = pltpu.make_async_copy(ids_ref.at[core], id_in.at[core], load_sem.at[1])
+    own_x = pltpu.make_async_copy(part_ref.at[core], x_in.at[0], load_sem.at[0])
+    own_id = pltpu.make_async_copy(ids_ref.at[core], id_in.at[0], load_sem.at[1])
     own_x.start()
     own_id.start()
 
@@ -108,54 +108,60 @@
         return carry
 
     lax.fori_loop(0, SECTIONS, greet, 0)
-    pl.semaphore_wait(barrier, SECTIONS * nz + 1)
-
     swap_x = pltpu.make_async_remote_copy(
-        src_ref=part_ref.at[other], dst_ref=x_in.at[core], send_sem=swap_send.at[0], recv_sem=swap_recv.at[0],
+        src_ref=part_ref.at[other], dst_ref=x_in.at[1], send_sem=swap_send.at[0], recv_sem=swap_recv.at[0],
         device_id=peer, device_id_type=MESH,
     )
     swap_id = pltpu.make_async_remote_copy(
-        src_ref=ids_ref.at[other], dst_ref=id_in.at[core], send_sem=swap_send.at[1], recv_sem=swap_recv.at[1],
+        src_ref=ids_ref.at[other], dst_ref=id_in.at[1], send_sem=swap_send.at[1], recv_sem=swap_recv.at[1],
         device_id=peer, device_id_type=MESH,
     )
+    slot_id = (lax.broadcasted_iota(jnp.int32, (128, 128), 1) & (SLICES - 1)).astype(jnp.float32)
+    parts = groups // 2
+
+    def take(h):
+        first = h * half_tiles
+
+        def unpack(i, carry):
+            for t in range(half_tiles):
+                tiles[pl.ds((first + t) * 8, comps), :] = x_in[h, i, :, 128 * t : 128 * (t + 1)]
+            for c in range(comps):
+                for g in range(h * parts, (h + 1) * parts):
+                    state[i, c, 8 * g : 8 * g + 8, :] = tiles[pl.ds(64 * g + c, 8, stride=8), :]
+            return carry
+
+        def build(i, carry):
+            columns = jnp.transpose(id_dense[i])
+            for t in range(first, first + half_tiles):
+                onehot[i, 128 * t : 128 * (t + 1), :] = bf(jnp.where(columns[:, t : t + 1] == slot_id, 1.0, 0.0))
+            return carry
+
+        lax.fori_loop(0, bunches, unpack, 0)
+        for t in range(half_tiles):
+            tiles[pl.ds((first + t) * 8, bunches), :] = id_in[h, :, 128 * t : 128 * (t + 1)].astype(jnp.float32)
+        for i in range(bunches):
+            for g in range(h * parts, (h + 1) * parts):
+                id_dense[i, 8 * g : 8 * g + 8, :] = tiles[pl.ds(64 * g + i, 8, stride=8), :]
+        lax.fori_loop(0, bunches, build, 0)
+
+    own_x.wait()
+    own_id.wait()
+    for i in range(bunches):
+        id_dense[i] = jnp.zeros((ntile, 128), jnp.float32)
+    take(0)
+    pl.semaphore_wait(barrier, SECTIONS * nz + 1)
     swap_id.start()
     swap_x.start()
-    own_x.wait()
-    own_id.wait()
+    mom_bf[...] = jnp.ones(mom_bf.shape, jnp.bfloat16)
     swap_id.wait()
     swap_x.wait()
-
-    def unpack(i, carry):
-        for h in range(2):
-            for t in range(half_tiles):
-                tiles[pl.ds((h * half_tiles + t) * 8, comps), :] = x_in[h, i, :, 128 * t : 128 * (t + 1)]
-        for c in range(comps):
-            for g in range(groups):
-                state[i, c, 8 * g : 8 * g + 8, :] = tiles[pl.ds(64 * g + c, 8, stride=8), :]
-        return carry
-
-    lax.fori_loop(0, bunches, unpack, 0)
-    for h in range(2):
-        for t in range(half_tiles):
-            tiles[pl.ds((h * half_tiles + t) * 8, bunches), :] = id_in[h, :, 128 * t : 128 * (t + 1)].astype(jnp.float32)
-    for i in range(bunches):
-        for g in range(groups):
-            id_dense[i, 8 * g : 8 * g + 8, :] = tiles[pl.ds(64 * g + i, 8, stride=8), :]
-
-    mom_bf[...] = jnp.ones(mom_bf.shape, jnp.bfloat16)
-    slot = (lax.broadcasted_iota(jnp.int32, (128, 128), 1) & (SLICES - 1)).astype(jnp.float32)
-
-    def build(i, carry):
-        columns = jnp.transpose(id_dense[i])
-        for t in range(ntile):
-            onehot[i, 128 * t : 128 * (t + 1), :] = bf(
-                jnp.where(columns[:, t : t + 1] == slot, 1.0, 0.0)
-            )
+    take(1)
+
+    def count(i, carry):
         counts[i] = jnp.dot(mom_bf[...], onehot[i], preferred_element_type=jnp.float32)[:8]
         return carry
 
-    lax.fori_loop(0, bunches, build, 0)
-
+    lax.fori_loop(0, bunches, count, 0)
     for g in range(groups):
         kick_rows[pl.ds(64 * g + 7, 8, stride=8), :] = jnp.zeros((8, 128), jnp.float32)
     low = lax.broadcasted_iota(jnp.int32, (8, 128), 1) < SLICES
@@ -275,11 +281,11 @@
     lax.fori_loop(0, STEPS - 1, cycle, 0)
 
     def own_out(i):
-        return pltpu.make_async_copy(x_out.at[core, i], out_ref.at[core, i], out_sem.at[i])
+        return pltpu.make_async_copy(x_out.at[0, i], out_ref.at[core, i], out_sem.at[i])
 
     def swap_out(i):
         return pltpu.make_async_remote_copy(
-            src_ref=x_out.at[other, i], dst_ref=out_ref.at[core, i], send_sem=out_send.at[i], recv_sem=out_recv.at[i],
+            src_ref=x_out.at[1, i], dst_ref=out_ref.at[core, i], send_sem=out_send.at[i], recv_sem=out_recv.at[i],
             device_id=peer, device_id_type=MESH,
         )
 
@@ -334,16 +340,16 @@
             vmem((2, bunches, width), jnp.int32),
             vmem((2, bunches, comps, width), f32),
             vmem((bunches, comps, ntile, 128), f32),
-            vmem((8 * ntile, 128), f32),
+            vmem((8 * ntile + 8, 128), f32),
             vmem((bunches, ntile, 128), f32),
             vmem((bunches, 2 * width, 128), b16),
             vmem((bunches, 8, 128), f32),
-            vmem((8 * ntile, 128), f32),
+            vmem((8 * ntile + 8, 128), f32),
             vmem((16, 2 * width), b16),
-            vmem((8 * ntile, 128), f32),
+            vmem((8 * ntile + 8, 128), f32),
             vmem((bunches, 16, 2 * width), b16),
-            vmem((8 * ntile, 128), f32),
-            vmem((8 * ntile, 128), f32),
+            vmem((8 * ntile + 8, 128), f32),
+            vmem((8 * ntile + 8, 128), f32),
             vmem((slots, 8, 128), f32),
             vmem((slots, nz, 8, 128), f32),
             vmem((comps, ntile, 128), f32),

time: 133 us -> 132 us (level)
    pallas_call x1, Pallas kernels: 129 us -> 128 us  [body(): pl.pallas_call(functools.partial(kernel, nb, nz, float(width * nd)), out_...]
where the time goes in v3:
time: 132 us; the launch traced here: 131 us
  Pallas kernels  128 us (97%)
  local copies, waits for them, and re-layouts  3.33 us (3%)
    pallas_call x1, Pallas kernels, body(): pl.pallas_call(functools.partial(kernel, nb, nz, float(width * nd)), out_...  128 us

profile of v3, /device:TPU:9, one launch (start us, length us, event | category | flops | bytes accessed | tf_op | source)
XLA Modules:
  0.0 131.4 jit_solution(15069373151911118318)
XLA Ops:
  0.0 0.9 copy.7
  0.9 0.1 reshape.3.maps_ref
  1.1 0.0 copy-start
  1.1 0.0 copy-start.1
  1.1 1.3 copy.8.part_ref
  2.3 0.0 copy-done
  2.4 0.0 copy-done.1
  2.4 128.0 %track.1 = f32[2,4,6,2048]{3,2,1,0:T(8,128)S(1)} custom-call(f32[2,4,6,2048]{3,2,1,0:T(8,128)S(1)} %copy.8.part_ref, s32[2,4,2048]{2,1,0:T(4,128)S(1)} %copy-done, f32[576]{0:T(1024)S(1)} %reshape.3.maps_ref, f32[2,8]{1,0:T(2,128)S(1)} %copy-done.1), custom_call_target="tpu_custom_call" | custom-call | tf_op jit(solution)/shard_map/track/pallas_call | solution.py:328
  130.4 1.0 copy.9
Async XLA Ops:
  1.1 1.3 copy-start
  1.1 1.3 copy-start.1
